TPU v7x, 256 devices: a whole 4x4x8 slice. The times are simulated.
256 devices in a mesh: gx: 16 (over y_lo, z), gz: 16 (over y_hi, x, core).
Axes of the slice: x: 4, y: 4 (y_hi: 2, y_lo: 2; y = y_hi * 2 + y_lo), z: 8, core: 2. Of those that a mesh axis runs over, the one named last changes fastest.
Arguments:
- temp: float32 [256, 1024, 256], P('gz', 'gx'), may hold values from -6 to 6
- u_vel: float32 [256, 1024, 256], P('gz', 'gx'), may hold values from -1.8 to 1.8
- v_vel: float32 [256, 1024, 256], P('gz', 'gx'), may hold values from -1.8 to 1.8
- w_vel: float32 [256, 1024, 256], P('gz', 'gx'), may hold values from -1.8 to 1.8
- temp_prev_tend: float32 [256, 1024, 256], P('gz', 'gx'), may hold values from -6 to 6
- w_prev_tend: float32 [256, 1024, 256], P('gz', 'gx'), may hold values from -6 to 6
- lower_coupling: float32 [256], P('gz'), may hold values from 256 to 4096
- upper_coupling: float32 [256], P('gz'), may hold values from 256 to 4096, as said below
- vertical_metric: float32 [256], P('gz'), may hold values from 0.25 to 2
Outputs:
- temp_next: float32 [256, 1024, 256], P('gz', 'gx')
- w_next: float32 [256, 1024, 256], P('gz', 'gx')
- temp_tend: float32 [256, 1024, 256], P('gz', 'gx')
- w_tend: float32 [256, 1024, 256], P('gz', 'gx')
Inputs may be any that keep to these rules, and one draw needn't show every extreme that they name: upper_coupling[k] equals lower_coupling[k + 1] for k < 255: the face shared by two levels.
All inputs are finite; a program needn't handle non-finite values.
Results may differ from a plain program's by a relative error of at most 0.0003.
Values sent between devices are 32-bit elements; how exact they have to be, the bound alone decides.
A program may use at most 128 MiB of HBM per device.

v0:
```python
import jax
import jax.numpy as jnp
from jax import lax
from jax.sharding import PartitionSpec as P

NEW_WEIGHT = 5.0 / 12.0
OLD_WEIGHT = -17.0 / 60.0
HORIZ_DIFF = 0.1


def padded(cells, sides, width, closed):
    for axis, dim in sides:
        count = lax.axis_size(axis)
        ends = count if closed else count - 1
        head = lax.slice_in_dim(cells, 0, width, axis=dim)
        tail = lax.slice_in_dim(cells, cells.shape[dim] - width, cells.shape[dim], axis=dim)
        cells = jnp.concatenate(
            [
                lax.ppermute(tail, axis, [(i, (i + 1) % count) for i in range(ends)]),
                cells,
                lax.ppermute(head, axis, [((i + 1) % count, i) for i in range(ends)]),
            ],
            axis=dim,
        )
    return cells


def shifted(array, axis, by):
    devices = lax.axis_size(axis)
    pairs = [(i, i + by) for i in range(devices) if 0 <= i + by < devices]
    return lax.ppermute(array, axis, pairs)


def sweep_solve(low_band, main_band, high_band, right_side):

    def forward(carry, row):
        ratio_prev, value_prev = carry
        low_val, main_val, high_val, rhs_row = row
        pivot_val = main_val - low_val * ratio_prev
        ratio_new = high_val / pivot_val
        value_new = (rhs_row - low_val * value_prev) / pivot_val
        return ((ratio_new, value_new), (ratio_new, value_new))

    start = (jnp.zeros((), jnp.float32), jnp.zeros(right_side.shape[1:], jnp.float32))
    _, (ratios, values) = lax.scan(
        forward, start, (low_band, main_band, high_band, right_side), unroll=True
    )

    def backward(next_value, row):
        ratio_row, value_row = row
        solved_row = value_row - ratio_row * next_value
        return (solved_row, solved_row)

    _, solved = lax.scan(
        backward,
        jnp.zeros(right_side.shape[1:], jnp.float32),
        (ratios, values),
        reverse=True,
        unroll=True,
    )
    return solved


def local(
    temp,
    u_vel,
    v_vel,
    w_vel,
    temp_prev_tend,
    w_prev_tend,
    lower_coupling,
    upper_coupling,
    vertical_metric,
):
    levels = temp.shape[0]
    inner_rows = levels - 1
    fields = jnp.stack((temp, w_vel))
    side_rim = padded(jnp.stack((temp, w_vel, u_vel)), (("gx", 2),), 1, True)
    wall_rim = padded(fields, (("gz", 1),), 1, False)
    flux_x = side_rim[:2] * side_rim[2:3]
    advect = 0.5 * (flux_x[:, :, 2:] - flux_x[:, :, :-2])
    flux_y = fields * v_vel
    advect = advect + 0.5 * (jnp.roll(flux_y, -1, 3) - jnp.roll(flux_y, 1, 3))
    flux_z = wall_rim * wall_rim[1:2]
    advect = advect + vertical_metric[:, None, None] * (flux_z[:, 2:] - flux_z[:, :-2])
    spread = (
        side_rim[:2, :, 2:]
        + side_rim[:2, :, :-2]
        + jnp.roll(fields, -1, 3)
        + jnp.roll(fields, 1, 3)
        - 4.0 * fields
    )
    tendency = -advect + HORIZ_DIFF * spread + jnp.stack((w_vel, temp))
    upper_face = upper_coupling[:, None, None]
    lower_face = lower_coupling[:, None, None]
    vertical = upper_face * (wall_rim[:, 2:] - fields) - lower_face * (fields - wall_rim[:, :-2])
    right_side = (
        fields
        + vertical
        + NEW_WEIGHT * tendency
        + OLD_WEIGHT * jnp.stack((temp_prev_tend, w_prev_tend))
    )
    inverse = sweep_solve(
        -lower_coupling[:inner_rows],
        1.0 + lower_coupling[:inner_rows] + upper_coupling[:inner_rows],
        -upper_coupling[:inner_rows],
        jnp.eye(inner_rows, dtype=jnp.float32),
    )
    partial_value = jnp.einsum(
        "kj,fjxy->fkxy", inverse, right_side[:, :inner_rows], precision=lax.Precision.HIGHEST
    )
    low_spike = lower_coupling[0] * inverse[:, 0]
    top_spike = upper_coupling[inner_rows - 1] * inverse[:, inner_rows - 1]
    head_above, low_above, top_above = shifted(
        (partial_value[:, 0], low_spike[0], top_spike[0]), "gz", -1
    )
    face_below = lower_coupling[levels - 1]
    face_above = upper_coupling[levels - 1]
    sub_here = -face_below * low_spike[inner_rows - 1]
    diag_here = (
        1.0
        + face_below
        + face_above
        - face_below * top_spike[inner_rows - 1]
        - face_above * low_above
    )
    sup_here = -face_above * top_above
    reduced = (
        right_side[:, levels - 1]
        + face_below * partial_value[:, inner_rows - 1]
        + face_above * head_above
    )
    position = lax.axis_index("gz")
    all_sub, all_diag, all_sup, all_rhs = (
        lax.all_gather(sub_here[None], "gz", axis=0, tiled=True),
        lax.all_gather(diag_here[None], "gz", axis=0, tiled=True),
        lax.all_gather(sup_here[None], "gz", axis=0, tiled=True),
        lax.all_gather(reduced[None], "gz", axis=0, tiled=True),
    )
    separators = sweep_solve(all_sub, all_diag, all_sup, all_rhs)
    own_value = lax.dynamic_index_in_dim(separators, position, 0, keepdims=False)
    below_value = lax.dynamic_index_in_dim(
        separators, jnp.maximum(position - 1, 0), 0, keepdims=False
    )
    below_value = jnp.where(position > 0, below_value, jnp.zeros_like(below_value))
    interior = (
        partial_value
        + low_spike[None, :, None, None] * below_value[:, None]
        + top_spike[None, :, None, None] * own_value[:, None]
    )
    solved = jnp.concatenate((interior, own_value[:, None]), axis=1)
    return (solved[0], solved[1], tendency[0], tendency[1])


def solution(mesh):
    return jax.shard_map(
        local,
        mesh=mesh,
        in_specs=(
            P("gz", "gx", None),
            P("gz", "gx", None),
            P("gz", "gx", None),
            P("gz", "gx", None),
            P("gz", "gx", None),
            P("gz", "gx", None),
            P("gz"),
            P("gz"),
            P("gz"),
        ),
        out_specs=(
            P("gz", "gx", None),
            P("gz", "gx", None),
            P("gz", "gx", None),
            P("gz", "gx", None),
        ),
        check_vma=False,
    )
```

profile of v0, /device:TPU:16, one launch (start us, length us, event | category | flops | bytes accessed | tf_op | source)
XLA Modules:
  0.0 224.3 jit_solution(17943546448327498601)
XLA Ops:
  7.2 0.0 all-gather.3.cloned.1.call-start
  7.2 2.0 copy.56
  9.2 1.2 copy_bitcast_fusion.4
  10.5 0.0 copy-start
  10.5 0.6 pad_maximum_fusion.14
  11.1 1.9 collective-permute-start.2
  13.0 4.7 %collective-permute-start.3 = (f32[3,16,1,256]{3,1,2,0:T(8,128)}, f32[3,16,1,256]{3,1,2,0:T(8,128)S(1)}, u32[]{:S(2)}, u32[]{:S(2)}) collective-permute-start(f32[3,16,1,256]{3,1,2,0:T(8,128)} %get-tuple-element.69), channel_id=1, source_target_pairs={{16,0},{32,16},{48,32},{64,48},{80,64},{96,80},{112,96},{128,112},... | collective-permute-start | bytes 147464 | tf_op jit(solution)/shard_map/ppermute | solution.py:21
  17.7 0.9 fusion.31
  18.6 3.9 %collective-permute-start = (f32[2,1,64,256]{3,1,2,0:T(1,128)}, f32[2,1,64,256]{3,1,2,0:T(1,128)S(1)}, u32[]{:S(2)}, u32[]{:S(2)}) collective-permute-start(f32[2,1,64,256]{3,1,2,0:T(1,128)} %get-tuple-element.86), channel_id=1, source_target_pairs={{1,0},{2,1},{3,2},{4,3},{5,4},{6,5},{7,6},{8,7},{9,8},{10,9},{11,1... | collective-permute-start | bytes 393224 | tf_op jit(solution)/shard_map/ppermute | solution.py:21
  22.5 1.9 collective-permute-start.1
  24.4 0.6 copy.36
  25.1 0.4 fusion.25
  25.4 2.8 %fusion.115 = (f32[2,16,64,255]{3,1,2,0:T(8,128)}, f32[2,16,64,255]{3,1,2,0:T(8,128)}) fusion(f32[2,16,64,256]{3,1,2,0:T(8,128)S(1)} %fusion.25), kind=kLoop, calls=%fused_computation.222 | loop fusion | bytes 8355840 | tf_op jit(solution)/shard_map/jit(_roll_static)/slice | solution.py:83
  28.2 1.6 fusion.116
  29.8 2.7 %fusion = (f32[2,16,64,255]{3,1,2,0:T(8,128)}, f32[2,16,64,255]{3,1,2,0:T(8,128)}) fusion(f32[1,16,64,256]{3,1,2,0:T(8,128)S(1)} %get-tuple-element.199, f32[1,16,64,256]{3,1,2,0:T(8,128)S(1)} %get-tuple-element.198), kind=kLoop, calls=%fused_computation.16 | loop fusion | flops 1044480 | bytes 6275072 | tf_op jit(solution)/shard_map/stack | solution.py:77
  32.6 1.7 fusion.28
  34.2 0.7 fusion.122
  34.9 0.7 fusion.124
  35.6 0.7 fusion.125
  36.3 0.7 fusion.126
  62.6 8.8 %fusion.76 = (f32[1,15]{1,0:T(1,128)S(1)}, f32[1,15]{1,0:T(1,128)S(1)}, f32[1,15]{1,0:T(1,128)S(1)}, f32[1,15]{1,0:T(1,128)S(1)}, f32[1,15]{1,0:T(1,128)S(1)}, /...) fusion(f32[15,15]{1,0:T(8,128)S(1)} %fusion.74, ...), kind=kLoop, calls=%fused_computation.175 | loop fusion | flops 615 | bytes 1792 | tf_op jit(solution)/shard_map/eval_jaxpr/div | solution.py:41
  74.1 4.1 %copy_bitcast_fusion.1 = (f32[1,16,64,256]{3,1,2,0:T(8,128)}, f32[1,16,64,256]{3,1,2,0:T(8,128)}) fusion(f32[16,64,256]{2,1,0:T(8,128)} %param.14, f32[16,64,256]{2,1,0:T(8,128)} %param.13), kind=kLoop, calls=%fused_computation.71 | loop fusion | bytes 4194304 | tf_op jit(solution)/shard_map/stack | solution.py:101
  78.2 1.4 multiply_subtract_fusion.14
  79.6 0.6 fusion.123
  80.2 1.4 concatenate.51
  81.7 0.0 collective-permute-done.2
  81.7 0.3 pad_maximum_fusion.1
  82.0 0.1 maximum_bitcast_fusion
  82.1 0.4 slice_multiply_fusion
  82.5 0.5 pad_maximum_fusion.2
  83.0 0.1 slice_bitcast_fusion
  83.1 0.0 copy-start.11
  83.1 0.6 broadcast_multiply_fusion
  83.7 0.0 copy-done.11
  83.8 9.1 %fusion.21 = (f32[2,16,64,256]{3,1,2,0:T(8,128)}, f32[2,16,64,256]{3,1,2,0:T(8,128)}) fusion(f32[2,1,64,256]{3,1,2,0:T(1,128)S(1)} %collective-permute-done.1, f32[1,16,64,256]{3,1,2,0:T(8,128)S(1)} %get-tuple-element.198, f32[1,16,64,256]{3,1,2,0:T(8,128)S(1)} %get-tuple-element.199, f32[2,1,64,256]{3,1,2,0:T(1,128)S(1)} %collective-permute-done, ...), kind=kLoop, calls=%fused_computation.46 | loop fusion | flops 22544384 | bytes 26575040 | tf_op jit(solution)/shard_map/add | solution.py:98
  92.9 3.5 %fusion.2 = f32[2,64,256,15]{2,3,1,0:T(8,128)S(1)} fusion(f32[2,16,64,256]{3,1,2,0:T(8,128)} %get-tuple-element.67, f32[15,15]{1,0:T(8,128)S(1)} %concatenate.51), kind=kOutput, calls=%fused_computation.18 | convolution fusion | flops 88473600 | bytes 4064132 | tf_op jit(solution)/shard_map/kj,fjxy->fkxy/dot_general | solution.py:109
  96.3 0.0 copy-start.12
  96.4 1.1 copy.55
  97.5 0.7 slice_bitcast_fusion.18
  98.2 7.3 %collective-permute-start.4 = (f32[2,64,256]{2,1,0:T(8,128)S(1)}, f32[2,64,256]{2,1,0:T(8,128)S(1)}, u32[]{:S(2)}, u32[]{:S(2)}) collective-permute-start(f32[2,64,256]{2,1,0:T(8,128)S(1)} %get-tuple-element.88), channel_id=1, source_target_pairs={{1,0},{2,1},{3,2},{4,3},{5,4},{6,5},{7,6},{8,7},{9,8},{10,9},{11,1... | collective-permute-start | bytes 393224 | tf_op jit(solution)/shard_map/ppermute | solution.py:31
  105.5 1.4 slice_add_fusion
  106.9 1.1 collective-permute-done.4
  108.0 1.3 bitcast_add_fusion
  109.3 0.0 all-gather.3.cloned.1.call-update
  109.3 1.3 fusion.91
  110.7 0.5 fusion.117
  111.2 7.4 %collective-permute-start.5 = (f32[]{:T(128)}, f32[]{:T(128)}, u32[]{:S(2)}, u32[]{:S(2)}) collective-permute-start(f32[]{:T(128)} %bitcast.65), channel_id=1, source_target_pairs={{1,0},{2,1},{3,2},{4,3},{5,4},{6,5},{7,6},{8,7},{9,8},{10,9},{11,1... | collective-permute-start | bytes 20 | tf_op jit(solution)/shard_map/ppermute | solution.py:31
  118.6 1.9 collective-permute-start.6
  124.5 0.6 dynamic-slice
  125.8 0.7 dynamic-update-slice
  127.8 0.7 dynamic-update-slice.1
  129.1 0.7 dynamic-update-slice.2
  129.8 33.8 %all-reduce.3 = (f32[16]{0:T(128)S(1)}, f32[16]{0:T(128)S(1)}, f32[16]{0:T(128)S(1)}) all-reduce(f32[16]{0:T(128)S(1)} %dynamic-update-slice.2, f32[16]{0:T(128)S(1)} %dynamic-update-slice.1, f32[16]{0:T(128)S(1)} %dynamic-update-slice), channel_id=1, replica_groups=mesh['gx'=16,'gz'=16] {'gz'}, use_global_device_ids=true, to_apply=%add.2 | all-reduce | flops 48 | bytes 384
  163.6 0.7 fusion.119
  164.9 0.7 fusion.120
  166.2 0.7 fusion.121
  195.6 1.7 slice_bitcast_fusion.1
  197.3 1.6 copy.41
  198.9 1.6 copy.42
  200.4 11.1 %subtract_dynamic-update-slice_fusion = (f32[16,2,64,256]{3,2,1,0:T(8,128)S(1)}, f32[1,2,64,256]{3,2,1,0:T(8,128)S(1)}, f32[1,2,64,256]{3,2,1,0:T(8,128)S(1)}, f...) fusion(f32[32,64,256]{2,1,0:T(8,128)} %all-gather.3.cloned.1.ca, ...), kind=kLoop, calls=%fused_computation.132 | loop fusion | flops 2555903 | bytes 4063424
  211.8 1.5 fusion.66
  213.3 1.5 constant_dynamic-update-slice_fusion
  214.9 1.2 multiply_add_fusion
  216.0 1.5 fusion.30
  (47 shorter events, 0.3 us)
Async XLA Ops:
  7.2 193.3 %all-gather.3.cloned.1.call-start = ((), (), s32[]{:S(2)}) async-start(), calls=%async_computation | async-start | bytes 2228224 | tf_op jit(solution)/shard_map/all_gather | solution.py:138
  7.2 2.0 copy-start.1
  7.2 2.0 copy-start.2
  10.5 14.0 %copy-start = (f32[16,64,256]{2,1,0:T(8,128)S(1)}, f32[16,64,256]{2,1,0:T(8,128)}, u32[]{:S(2)}) copy-start(f32[16,64,256]{2,1,0:T(8,128)} %param.11) | copy-start | bytes 3145732
  11.1 70.6 %collective-permute-start.2 = (f32[3,16,1,256]{3,1,2,0:T(8,128)}, f32[3,16,1,256]{3,1,2,0:T(8,128)S(1)}, u32[]{:S(2)}, u32[]{:S(2)}) collective-permute-start(f32[3,16,1,256]{3,1,2,0:T(8,128)} %get-tuple-element.70), channel_id=1, source_target_pairs={{0,16},{16,32},{32,48},{48,64},{64,80},{80,96},{96,112},{112,128},... | collective-permute-start | bytes 147464 | tf_op jit(solution)/shard_map/ppermute | solution.py:19
  13.0 68.7 %collective-permute-start.3 = (f32[3,16,1,256]{3,1,2,0:T(8,128)}, f32[3,16,1,256]{3,1,2,0:T(8,128)S(1)}, u32[]{:S(2)}, u32[]{:S(2)}) collective-permute-start(f32[3,16,1,256]{3,1,2,0:T(8,128)} %get-tuple-element.69), channel_id=1, source_target_pairs={{16,0},{32,16},{48,32},{64,48},{80,64},{96,80},{112,96},{128,112},... | collective-permute-start | bytes 147464 | tf_op jit(solution)/shard_map/ppermute | solution.py:21
  18.6 63.9 %collective-permute-start = (f32[2,1,64,256]{3,1,2,0:T(1,128)}, f32[2,1,64,256]{3,1,2,0:T(1,128)S(1)}, u32[]{:S(2)}, u32[]{:S(2)}) collective-permute-start(f32[2,1,64,256]{3,1,2,0:T(1,128)} %get-tuple-element.86), channel_id=1, source_target_pairs={{1,0},{2,1},{3,2},{4,3},{5,4},{6,5},{7,6},{8,7},{9,8},{10,9},{11,1... | collective-permute-start | bytes 393224 | tf_op jit(solution)/shard_map/ppermute | solution.py:21
  22.5 60.0 %collective-permute-start.1 = (f32[2,1,64,256]{3,1,2,0:T(1,128)}, f32[2,1,64,256]{3,1,2,0:T(1,128)S(1)}, u32[]{:S(2)}, u32[]{:S(2)}) collective-permute-start(f32[2,1,64,256]{3,1,2,0:T(1,128)} %get-tuple-element.87), channel_id=1, source_target_pairs={{0,1},{1,2},{2,3},{3,4},{4,5},{5,6},{6,7},{7,8},{8,9},{9,10},{10,1... | collective-permute-start | bytes 393224 | tf_op jit(solution)/shard_map/ppermute | solution.py:19
  32.6 1.7 copy-start.3
  32.6 2.3 %copy-start.4 = (f32[16]{0:T(128)S(1)}, f32[16]{0:T(128)}, u32[]{:S(2)}) copy-start(f32[16]{0:T(128)} %param.16) | copy-start | bytes 196
  74.1 4.1 %copy-start.5 = (f32[1,15]{1,0:T(1,128)S(1)}, f32[1,15]{1,0:T(1,128)}, u32[]{:S(2)}) copy-start(f32[1,15]{1,0:T(1,128)} %get-tuple-element.61) | copy-start | bytes 184
  74.1 4.1 %copy-start.6 = (f32[1,15]{1,0:T(1,128)S(1)}, f32[1,15]{1,0:T(1,128)}, u32[]{:S(2)}) copy-start(f32[1,15]{1,0:T(1,128)} %get-tuple-element.62) | copy-start | bytes 184
  74.1 4.1 %copy-start.7 = (f32[1,15]{1,0:T(1,128)S(1)}, f32[1,15]{1,0:T(1,128)}, u32[]{:S(2)}) copy-start(f32[1,15]{1,0:T(1,128)} %get-tuple-element.63) | copy-start | bytes 184
  74.1 4.1 %copy-start.8 = (f32[1,15]{1,0:T(1,128)S(1)}, f32[1,15]{1,0:T(1,128)}, u32[]{:S(2)}) copy-start(f32[1,15]{1,0:T(1,128)} %get-tuple-element.64) | copy-start | bytes 184
  74.1 4.1 %copy-start.9 = (f32[1,15]{1,0:T(1,128)S(1)}, f32[1,15]{1,0:T(1,128)}, u32[]{:S(2)}) copy-start(f32[1,15]{1,0:T(1,128)} %get-tuple-element.65) | copy-start | bytes 184
  74.1 4.1 %copy-start.10 = (f32[1,15]{1,0:T(1,128)S(1)}, f32[1,15]{1,0:T(1,128)}, u32[]{:S(2)}) copy-start(f32[1,15]{1,0:T(1,128)} %get-tuple-element.66) | copy-start | bytes 184
  83.1 0.7 copy-start.11
  96.3 28.2 %copy-start.12 = (u32[256]{0:T(256)S(1)}, u32[256]{0:T(256)}, u32[]{:S(2)}) copy-start(u32[256]{0:T(256)} %constant.39) | copy-start | bytes 3076
  98.2 9.8 %collective-permute-start.4 = (f32[2,64,256]{2,1,0:T(8,128)S(1)}, f32[2,64,256]{2,1,0:T(8,128)S(1)}, u32[]{:S(2)}, u32[]{:S(2)}) collective-permute-start(f32[2,64,256]{2,1,0:T(8,128)S(1)} %get-tuple-element.88), channel_id=1, source_target_pairs={{1,0},{2,1},{3,2},{4,3},{5,4},{6,5},{7,6},{8,7},{9,8},{10,9},{11,1... | collective-permute-start | bytes 393224 | tf_op jit(solution)/shard_map/ppermute | solution.py:31
  111.2 15.2 %collective-permute-start.5 = (f32[]{:T(128)}, f32[]{:T(128)}, u32[]{:S(2)}, u32[]{:S(2)}) collective-permute-start(f32[]{:T(128)} %bitcast.65), channel_id=1, source_target_pairs={{1,0},{2,1},{3,2},{4,3},{5,4},{6,5},{7,6},{8,7},{9,8},{10,9},{11,1... | collective-permute-start | bytes 20 | tf_op jit(solution)/shard_map/ppermute | solution.py:31
  118.6 9.8 %collective-permute-start.6 = (f32[]{:T(128)}, f32[]{:T(128)}, u32[]{:S(2)}, u32[]{:S(2)}) collective-permute-start(f32[]{:T(128)} %bitcast.69), channel_id=1, source_target_pairs={{1,0},{2,1},{3,2},{4,3},{5,4},{6,5},{7,6},{8,7},{9,8},{10,9},{11,1... | collective-permute-start | bytes 20 | tf_op jit(solution)/shard_map/ppermute | solution.py:31
Sparse Core Ops, SparseCore 0:
  109.5 50.9 all-gather.2
where the time goes:
time: 226 us; the launch traced here: 224 us
  between operations  79.1 us (35%)
  other arithmetic  49.1 us (22%)
  blocking collectives  33.8 us (15%)
  starting transfers between devices  29 us (13%)
  local copies, waits for them, and re-layouts  28.8 us (13%)
  matrix products  3.46 us (2%)
    unnamed x1, blocking collectives  33.8 us
    ppermute x3, starting transfers between devices, shifted(): return lax.ppermute(array, axis, pairs)  16.6 us
    unnamed x8, other arithmetic  12.7 us
    add x1, other arithmetic, local(): fields + vertical + NEW_WEIGHT * tendency  9.08 us
    div x1, other arithmetic, forward(): value_new = (rhs_row - low_val * value_prev) / pivot_val  8.84 us
    unnamed x44, local copies, waits for them, and re-layouts  8.54 us
    ppermute x2, starting transfers between devices, padded(): lax.ppermute(head, axis, [((i + 1) % count, i) for i in range(ends)])  8.54 us
    another operation x3, other arithmetic, local(): fields = jnp.stack((temp, w_vel))  5.29 us
  transfers between devices with their start and end apart: 8, of which 1 were waited for; matrix products, arithmetic and copies ran while one was open for 19% of the time, Pallas kernels for 0%

commit v1 on v0

v1 whole, which is shorter than its diff:
```python
import functools

import jax
import jax.numpy as jnp
from jax import lax
from jax.experimental import pallas as pl
from jax.experimental.pallas import tpu as pltpu
from jax.sharding import PartitionSpec as P

NEW_WEIGHT = 5.0 / 12.0
OLD_WEIGHT = -17.0 / 60.0
HORIZ_DIFF = 0.1
MESH = pl.DeviceIdType.MESH
PAD = 8


def exchange_kernel(
    n, temp, u_vel, v_vel, w_vel, temp_old, w_old, lower, upper, metric,
    part_t, part_w, tend_t, tend_w, state, basis,
    tbuf, ubuf, wbuf, vbuf, tobuf, wobuf,
    low_s, up_s, met_s,
    inv, mine, mats, edge_out, edge_lo, edge_hi, below, above,
    ends, gathered, sols, entry,
    load_sem, scal_sem, mat_send, mat_recv, edge_send, edge_recv, wall_send, wall_recv,
    fwd_send, fwd_recv, back_send, back_recv,
):
    levels, rows, cols = temp.shape
    halves = cols // 128
    blocks = rows // 8
    me = lax.axis_index("gz")
    gx = lax.axis_index("gx")
    nx = lax.axis_size("gx")
    right = lax.rem(gx + 1, nx)
    left = lax.rem(gx + nx - 1, nx)

    scal = [
        pltpu.make_async_copy(src, dst, scal_sem.at[i])
        for i, (src, dst) in enumerate(((lower, low_s), (upper, up_s), (metric, met_s)))
    ]
    for c in scal:
        c.start()
    loads = []
    for i, (src, dst) in enumerate(
        ((temp, tbuf), (w_vel, wbuf), (u_vel, ubuf), (v_vel, vbuf), (temp_old, tobuf), (w_old, wobuf))
    ):
        first = PAD if i < 3 else 0
        for h in range(halves):
            c = pltpu.make_async_copy(
                src.at[:, :, pl.ds(h * 128, 128)],
                dst.at[:, h, pl.ds(first, rows), :],
                load_sem.at[i, h],
            )
            c.start()
            loads.append(c)

    barrier = pltpu.get_barrier_semaphore()
    for step in range(1, n):
        pl.semaphore_signal(
            barrier, inc=1, device_id={"gz": lax.rem(me + step, n)}, device_id_type=MESH
        )
    for other in (left, right):
        pl.semaphore_signal(barrier, inc=1, device_id={"gx": other}, device_id_type=MESH)

    for c in scal:
        c.wait()
    one = jnp.ones((8, 128), jnp.float32)
    zero = jnp.zeros((8, 128), jnp.float32)
    phi, phi_flux, psi, psi_flux = one, zero, zero, one
    for k in range(levels):
        inv_k = 1.0 / (one * up_s[k])
        inv[k] = inv_k
        basis[0, k] = phi
        basis[1, k] = psi
        phi_flux = phi_flux + phi
        psi_flux = psi_flux + psi
        phi = phi + phi_flux * inv_k
        psi = psi + psi_flux * inv_k
    sub = lax.broadcasted_iota(jnp.int32, (8, 128), 0)
    mine[0] = phi
    mine[1] = psi
    mine[2] = phi_flux
    mine[3] = psi_flux
    mat = jnp.where(sub == 0, phi, zero)
    mat = jnp.where(sub == 1, psi, mat)
    mat = jnp.where(sub == 2, phi_flux, mat)
    mat = jnp.where(sub == 3, psi_flux, mat)
    mat = jnp.where(sub == 4, one * low_s[0], mat)
    mats[me] = mat

    pl.semaphore_wait(barrier, n + 1)

    up_copies = [
        pltpu.make_async_remote_copy(
            src_ref=src.at[levels - 1],
            dst_ref=below.at[i],
            send_sem=wall_send.at[0, i],
            recv_sem=wall_recv.at[0, i],
            device_id={"gz": lax.rem(me + 1, n)},
            device_id_type=MESH,
        )
        for i, src in enumerate((temp, w_vel))
    ]
    down_copies = [
        pltpu.make_async_remote_copy(
            src_ref=src.at[0],
            dst_ref=above.at[i],
            send_sem=wall_send.at[1, i],
            recv_sem=wall_recv.at[1, i],
            device_id={"gz": lax.rem(me + n - 1, n)},
            device_id_type=MESH,
        )
        for i, src in enumerate((temp, w_vel))
    ]

    @pl.when(me < n - 1)
    def _():
        for c in up_copies:
            c.start()

    @pl.when(me > 0)
    def _():
        for c in down_copies:
            c.start()

    @pl.when(me == 0)
    def _():
        below[...] = jnp.zeros_like(below)

    @pl.when(me == n - 1)
    def _():
        above[...] = jnp.zeros_like(above)

    def mat_copy(step):
        return pltpu.make_async_remote_copy(
            src_ref=mats.at[me],
            dst_ref=mats.at[me],
            send_sem=mat_send.at[step],
            recv_sem=mat_recv.at[step],
            device_id={"gz": lax.rem(me + step, n)},
            device_id_type=MESH,
        )

    for step in range(1, n):
        mat_copy(step).start()

    for c in loads[: 3 * halves]:
        c.wait()
    for k in range(levels):
        for a, buf in enumerate((tbuf, wbuf, ubuf)):
            for h in range(halves):
                edge_out[0, a, h, pl.ds(k, 1), :] = buf[k, h, pl.ds(PAD, 1), :]
                edge_out[1, a, h, pl.ds(k, 1), :] = buf[k, h, pl.ds(PAD + rows - 1, 1), :]
    to_left = pltpu.make_async_remote_copy(
        src_ref=edge_out.at[0], dst_ref=edge_hi, send_sem=edge_send.at[0], recv_sem=edge_recv.at[0],
        device_id={"gx": left}, device_id_type=MESH,
    )
    to_right = pltpu.make_async_remote_copy(
        src_ref=edge_out.at[1], dst_ref=edge_lo, send_sem=edge_send.at[1], recv_sem=edge_recv.at[1],
        device_id={"gx": right}, device_id_type=MESH,
    )
    to_left.start()
    to_right.start()
    for c in loads[3 * halves :]:
        c.wait()

    lane = lax.broadcasted_iota(jnp.int32, (8, 128), 1)
    first_lane = lane == 0
    last_lane = lane == 127

    def next_col(g):
        r = [pltpu.roll(x, 127, 1) for x in g]
        return [jnp.where(last_lane, r[(h + 1) % halves], r[h]) for h in range(halves)]

    def prev_col(g):
        r = [pltpu.roll(x, 1, 1) for x in g]
        return [jnp.where(first_lane, r[(h - 1) % halves], r[h]) for h in range(halves)]

    def block(step, carry):
        ib = jnp.where(step < blocks - 2, step + 1, jnp.where(step == blocks - 2, 0, blocks - 1))

        @pl.when(step == blocks - 2)
        def _():
            to_left.wait_recv()
            to_right.wait_recv()
            for k in range(levels):
                for a, buf in enumerate((tbuf, wbuf, ubuf)):
                    for h in range(halves):
                        buf[k, h, pl.ds(PAD - 1, 1), :] = edge_lo[a, h, pl.ds(k, 1), :]
                        buf[k, h, pl.ds(PAD + rows, 1), :] = edge_hi[a, h, pl.ds(k, 1), :]

        row = pl.multiple_of(ib * 8, 8)
        H = range(halves)

        def center(buf, k):
            return [buf[k, h, pl.ds(row + PAD, 8), :] for h in H]

        y = [[zero for _ in H] for _ in range(2)]
        flux = [[zero for _ in H] for _ in range(2)]
        f = [center(tbuf, 0), center(wbuf, 0)]
        wf = [[f[1][h] * f[q][h] for h in H] for q in range(2)]
        wf_below = [[zero for _ in H] for _ in range(2)]
        for k in range(levels):
            if k < levels - 1:
                f_up = [center(tbuf, k + 1), center(wbuf, k + 1)]
                wf_up = [[f_up[1][h] * f_up[q][h] for h in H] for q in range(2)]
            else:
                f_up, wf_up = None, [[zero for _ in H] for _ in range(2)]
            m_k = met_s[k]
            inv_k = inv[k]
            from_hi, from_lo, y_hi, y_lo = [], [], [], []
            for h in H:
                from_hi.append(HORIZ_DIFF - 0.5 * ubuf[k, h, pl.ds(row + PAD + 1, 8), :])
                from_lo.append(HORIZ_DIFF + 0.5 * ubuf[k, h, pl.ds(row + PAD - 1, 8), :])
                hv = 0.5 * vbuf[k, h, pl.ds(row, 8), :]
                y_hi.append(HORIZ_DIFF - hv)
                y_lo.append(HORIZ_DIFF + hv)
            for q, (buf, old, tend, part) in enumerate(
                ((tbuf, tobuf, tend_t, part_t), (wbuf, wobuf, tend_w, part_w))
            ):
                nxt = next_col([f[q][h] * y_hi[h] for h in H])
                prv = prev_col([f[q][h] * y_lo[h] for h in H])
                for h in H:
                    acc = (
                        buf[k, h, pl.ds(row + PAD + 1, 8), :] * from_hi[h]
                        + buf[k, h, pl.ds(row + PAD - 1, 8), :] * from_lo[h]
                    )
                    acc = acc + (nxt[h] + prv[h])
                    acc = acc + (f[1 - q][h] - (4.0 * HORIZ_DIFF) * f[q][h])
                    acc = acc + m_k * (wf_below[q][h] - wf_up[q][h])
                    tend[k, pl.ds(row, 8), pl.ds(h * 128, 128)] = acc
                    rhs = (
                        (f[q][h] + f[q][h])
                        + NEW_WEIGHT * acc
                        + OLD_WEIGHT * old[k, h, pl.ds(row, 8), :]
                    )
                    part[k, pl.ds(row, 8), pl.ds(h * 128, 128)] = y[q][h] - f[q][h]
                    flux[q][h] = flux[q][h] + (y[q][h] - rhs)
                    y[q][h] = y[q][h] + flux[q][h] * inv_k
            wf_below, wf, f = wf, wf_up, f_up
        for h in H:
            for q in range(2):
                ends[ib * halves + h, 2 * q] = y[q][h]
                ends[ib * halves + h, 2 * q + 1] = flux[q][h]
        return carry

    lax.fori_loop(0, blocks, block, 0)

    @pl.when(me > 0)
    def _():
        for c in up_copies:
            c.wait_recv()

    @pl.when(me < n - 1)
    def _():
        for c in down_copies:
            c.wait_recv()

    m_lo = NEW_WEIGHT * met_s[0]
    m_hi = NEW_WEIGHT * met_s[levels - 1]

    def fwd_copy(step):
        to = lax.rem(me + step, n)
        return pltpu.make_async_remote_copy(
            src_ref=ends.at[to],
            dst_ref=gathered.at[me],
            send_sem=fwd_send.at[step],
            recv_sem=fwd_recv.at[step],
            device_id={"gz": to},
            device_id_type=MESH,
        )

    def tile_of(buf, tile, q):
        r = pl.multiple_of((tile // halves) * 8, 8)
        c = pl.multiple_of(lax.rem(tile, halves) * 128, 128)
        return buf[q, pl.ds(r, 8), pl.ds(c, 128)]

    def fix(tile):
        for q in range(2):
            lo = m_lo * (tile_of(below, tile, 1) * tile_of(below, tile, q))
            hi = m_hi * (tile_of(above, tile, 1) * tile_of(above, tile, q))
            ends[tile, 2 * q] = ends[tile, 2 * q] - mine[1] * lo + inv[levels - 1] * hi
            ends[tile, 2 * q + 1] = ends[tile, 2 * q + 1] - mine[3] * lo + hi

    for step in range(1, n):
        fix(lax.rem(me + step, n))
        fwd_copy(step).start()
    fix(me)
    gathered[me] = ends[me]

    for q, tend in enumerate((tend_t, tend_w)):
        tend[0] = tend[0] + met_s[0] * (below[1] * below[q])
        tend[levels - 1] = tend[levels - 1] - met_s[levels - 1] * (above[1] * above[q])

    for step in range(1, n):
        mat_copy(step).wait_recv()

    def entry_of(d, r):
        return jnp.broadcast_to(mats[d, pl.ds(r, 1), :], (8, 128))

    bottom = [(one, entry_of(0, 4))]
    for d in range(n):
        a, b = bottom[-1]
        bottom.append(
            (entry_of(d, 0) * a + entry_of(d, 1) * b, entry_of(d, 2) * a + entry_of(d, 3) * b)
        )
    top = [(zero, one)]
    for d in range(n - 1, -1, -1):
        a, b = top[-1]
        top.append(
            (entry_of(d, 3) * a + entry_of(d, 1) * b, entry_of(d, 2) * a + entry_of(d, 0) * b)
        )
    top = top[::-1]
    scale = 1.0 / bottom[n][0]

    for step in range(1, n):
        fwd_copy(step).wait_recv()

    for q in range(2):
        amp = [None] * n
        run = zero
        for d in range(n - 1, -1, -1):
            a, b = top[d + 1]
            run = run - (gathered[d, 2 * q] * b + gathered[d, 2 * q + 1] * a)
            amp[d] = run * scale
        run = zero
        for d in range(n):
            bot, up = bottom[d], top[d]
            beta = run * scale
            sols[d, 2 * q] = bot[0] * amp[d] - up[0] * beta
            sols[d, 2 * q + 1] = bot[1] * amp[d] + up[1] * beta
            a, b = bottom[d + 1]
            run = run + (a * gathered[d, 2 * q + 1] - b * gathered[d, 2 * q])

    def back_copy(step):
        to = lax.rem(me + step, n)
        return pltpu.make_async_remote_copy(
            src_ref=sols.at[to],
            dst_ref=entry.at[me],
            send_sem=back_send.at[step],
            recv_sem=back_recv.at[step],
            device_id={"gz": to},
            device_id_type=MESH,
        )

    for step in range(1, n):
        back_copy(step).start()
    entry[me] = sols[me]
    for step in range(1, n):
        back_copy(step).wait_recv()
    for tile in range(n):
        r, c = 8 * (tile // halves), 128 * (tile % halves)
        for q in range(2):
            lo = m_lo * (
                below[1, pl.ds(r, 8), pl.ds(c, 128)] * below[q, pl.ds(r, 8), pl.ds(c, 128)]
            )
            state[2 * q, pl.ds(r, 8), pl.ds(c, 128)] = entry[tile, 2 * q]
            state[2 * q + 1, pl.ds(r, 8), pl.ds(c, 128)] = entry[tile, 2 * q + 1] - lo

    @pl.when(me < n - 1)
    def _():
        for c in up_copies:
            c.wait_send()

    @pl.when(me > 0)
    def _():
        for c in down_copies:
            c.wait_send()

    to_left.wait_send()
    to_right.wait_send()
    for step in range(1, n):
        mat_copy(step).wait_send()
        fwd_copy(step).wait_send()
        back_copy(step).wait_send()


def finish_kernel(
    part_t, part_w, tend_t, tend_w, state, basis,
    temp_next, w_next, tend_t_out, tend_w_out,
    xbuf, sems,
):
    levels, rows, cols = part_t.shape
    outs = [
        pltpu.make_async_copy(tend_t, tend_t_out, sems.at[0]),
        pltpu.make_async_copy(tend_w, tend_w_out, sems.at[1]),
    ]
    for c in outs:
        c.start()

    def level(k):
        phi = jnp.concatenate([basis[0, k]] * (cols // 128), axis=1)[:1]
        psi = jnp.concatenate([basis[1, k]] * (cols // 128), axis=1)[:1]
        for q, part in enumerate((part_t, part_w)):
            xbuf[q, k] = part[k] + phi * state[2 * q] + psi * state[2 * q + 1]

    for k in range(levels):
        level(k)
        for q, out in enumerate((temp_next, w_next)):
            c = pltpu.make_async_copy(xbuf.at[q, k], out.at[k], sems.at[2 + q * levels + k])
            c.start()
            outs.append(c)
    for c in outs:
        c.wait()


def local(n, temp, u_vel, v_vel, w_vel, temp_old, w_old, lower, upper, metric):
    levels, rows, cols = temp.shape
    halves = cols // 128
    f32 = jnp.float32
    cube = jax.ShapeDtypeStruct((levels, rows, cols), f32)
    hbm = pl.BlockSpec(memory_space=pltpu.HBM)
    vmem = pl.BlockSpec(memory_space=pltpu.VMEM)
    dma = pltpu.SemaphoreType.DMA
    padded = pltpu.VMEM((levels, halves, rows + 2 * PAD, 128), f32)
    plain = pltpu.VMEM((levels, halves, rows, 128), f32)
    edge = (3, halves, levels, 128)
    parts = pl.pallas_call(
        functools.partial(exchange_kernel, n),
        out_shape=(
            cube, cube, cube, cube,
            jax.ShapeDtypeStruct((4, rows, cols), f32),
            jax.ShapeDtypeStruct((2, levels, 8, 128), f32),
        ),
        in_specs=[hbm] * 9,
        out_specs=(vmem,) * 6,
        scratch_shapes=[
            padded, padded, padded, plain, plain, plain,
            pltpu.SMEM((levels,), f32), pltpu.SMEM((levels,), f32), pltpu.SMEM((levels,), f32),
            pltpu.VMEM((levels, 8, 128), f32),
            pltpu.VMEM((4, 8, 128), f32),
            pltpu.VMEM((n, 8, 128), f32),
            pltpu.VMEM((2, *edge), f32),
            pltpu.VMEM(edge, f32),
            pltpu.VMEM(edge, f32),
            pltpu.VMEM((2, rows, cols), f32),
            pltpu.VMEM((2, rows, cols), f32),
            pltpu.VMEM((n, 4, 8, 128), f32),
            pltpu.VMEM((n, 4, 8, 128), f32),
            pltpu.VMEM((n, 4, 8, 128), f32),
            pltpu.VMEM((n, 4, 8, 128), f32),
            dma((6, halves)), dma((3,)),
            dma((n,)), dma((n,)), dma((2,)), dma((2,)), dma((2, 2)), dma((2, 2)),
            dma((n,)), dma((n,)), dma((n,)), dma((n,)),
        ],
        compiler_params=pltpu.CompilerParams(
            collective_id=0, has_side_effects=True, vmem_limit_bytes=40 * 1024 * 1024
        ),
        name="exchange",
    )(
        *(
            pltpu.with_memory_space_constraint(x, pltpu.HBM)
            for x in (temp, u_vel, v_vel, w_vel, temp_old, w_old, lower, upper, metric)
        )
    )
    return pl.pallas_call(
        finish_kernel,
        out_shape=(cube,) * 4,
        in_specs=[vmem] * 6,
        out_specs=(hbm,) * 4,
        scratch_shapes=[pltpu.VMEM((2, levels, rows, cols), f32), dma((2 + 2 * levels,))],
        compiler_params=pltpu.CompilerParams(vmem_limit_bytes=24 * 1024 * 1024),
        name="finish",
    )(*parts)


def solution(mesh):
    cube = P("gz", "gx", None)
    line = P("gz")
    return jax.shard_map(
        functools.partial(local, mesh.shape["gz"]),
        mesh=mesh,
        in_specs=(cube,) * 6 + (line,) * 3,
        out_specs=(cube,) * 4,
        check_vma=False,
    )
```

time: 226 us -> 31.7 us (0.14)
  the two profiles are of different devices: /device:TPU:16 before, /device:TPU:1 now
where the time goes in v1:
time: 31.7 us; the launch traced here: 31.6 us
  Pallas kernels  31 us (98%)
  between operations  0.64 us (2%)
    pallas_call x1, Pallas kernels, local(): pl.pallas_call(functools.partial(exchange_kernel, n), out_shape=(cube, cu...  28.7 us
    pallas_call x1, Pallas kernels, local(): pl.pallas_call(finish_kernel, out_shape=(cube,) * 4, in_specs=[vmem] * 6,...  2.28 us

profile of v1, /device:TPU:1, one launch (start us, length us, event | category | flops | bytes accessed | tf_op | source)
XLA Modules:
  0.0 31.6 jit_solution(1762580462690279278)
XLA Ops:
  0.6 28.7 %exchange.1 = (f32[16,64,256]{2,1,0:T(8,128)S(1)}, f32[16,64,256]{2,1,0:T(8,128)S(1)}, f32[16,64,256]{2,1,0:T(8,128)S(1)}, f32[16,64,256]{2,1,0:T(8,128)S(1)}, f...) custom-call(f32[16,64,256]{2,1,0:T(8,128)} %temp.1, f32[16,64,256]{2,1,0:T(8,128)} %u_vel.1, ...), custom_call_target="tpu_custom_call" | custom-call | tf_op jit(solution)/shard_map/exchange/pallas_call | solution.py:417
  29.3 2.3 %finish.1 = (f32[16,64,256]{2,1,0:T(8,128)}, f32[16,64,256]{2,1,0:T(8,128)}, f32[16,64,256]{2,1,0:T(8,128)}, f32[16,64,256]{2,1,0:T(8,128)}) custom-call(f32[16,64,256]{2,1,0:T(8,128)S(1)} %get-tuple-element.10.part_t, f32[16,64,256]{2,1,0:T(8,128)S(1)} %get-tuple-element.11.part_w, f32[16,64,256]{2,1,0:T(8,128)S(1)} %get-tuple-element.12.tend_t, ...), custom_call_target="tpu_custom_call" | custom-call | tf_op jit(solution)/shard_map/finish/pallas_call | solution.py:455

commit v2 on v1

--- a/solution.py
+++ b/solution.py
@@ -85,9 +85,24 @@
     mat = jnp.where(sub == 2, phi_flux, mat)
     mat = jnp.where(sub == 3, psi_flux, mat)
     mat = jnp.where(sub == 4, one * low_s[0], mat)
+    mat = jnp.where(sub == 5, one * met_s[0], mat)
+    mat = jnp.where(sub == 6, one * met_s[levels - 1], mat)
     mats[me] = mat
 
     pl.semaphore_wait(barrier, n + 1)
+
+    def mat_copy(step):
+        return pltpu.make_async_remote_copy(
+            src_ref=mats.at[me],
+            dst_ref=mats.at[me],
+            send_sem=mat_send.at[step],
+            recv_sem=mat_recv.at[step],
+            device_id={"gz": lax.rem(me + step, n)},
+            device_id_type=MESH,
+        )
+
+    for step in (1, n - 1, *range(2, n - 1)):
+        mat_copy(step).start()
 
     up_copies = [
         pltpu.make_async_remote_copy(
@@ -129,19 +144,6 @@
     @pl.when(me == n - 1)
     def _():
         above[...] = jnp.zeros_like(above)
-
-    def mat_copy(step):
-        return pltpu.make_async_remote_copy(
-            src_ref=mats.at[me],
-            dst_ref=mats.at[me],
-            send_sem=mat_send.at[step],
-            recv_sem=mat_recv.at[step],
-            device_id={"gz": lax.rem(me + step, n)},
-            device_id_type=MESH,
-        )
-
-    for step in range(1, n):
-        mat_copy(step).start()
 
     for c in loads[: 3 * halves]:
         c.wait()
@@ -175,19 +177,7 @@
         r = [pltpu.roll(x, 1, 1) for x in g]
         return [jnp.where(first_lane, r[(h - 1) % halves], r[h]) for h in range(halves)]
 
-    def block(step, carry):
-        ib = jnp.where(step < blocks - 2, step + 1, jnp.where(step == blocks - 2, 0, blocks - 1))
-
-        @pl.when(step == blocks - 2)
-        def _():
-            to_left.wait_recv()
-            to_right.wait_recv()
-            for k in range(levels):
-                for a, buf in enumerate((tbuf, wbuf, ubuf)):
-                    for h in range(halves):
-                        buf[k, h, pl.ds(PAD - 1, 1), :] = edge_lo[a, h, pl.ds(k, 1), :]
-                        buf[k, h, pl.ds(PAD + rows, 1), :] = edge_hi[a, h, pl.ds(k, 1), :]
-
+    def block(ib):
         row = pl.multiple_of(ib * 8, 8)
         H = range(halves)
 
@@ -241,9 +231,86 @@
             for q in range(2):
                 ends[ib * halves + h, 2 * q] = y[q][h]
                 ends[ib * halves + h, 2 * q + 1] = flux[q][h]
+
+    def fwd_copy(tile, src, dst):
+        return pltpu.make_async_remote_copy(
+            src_ref=ends.at[tile],
+            dst_ref=gathered.at[src],
+            send_sem=fwd_send.at[dst],
+            recv_sem=fwd_recv.at[src],
+            device_id={"gz": dst},
+            device_id_type=MESH,
+        )
+
+    stride = 5
+
+    def fix_and_send(tile):
+        ib = tile // halves
+        h = lax.rem(tile, halves)
+        r = pl.multiple_of(ib * 8 + PAD, 8)
+        for q, buf in enumerate((tbuf, wbuf)):
+            lo = m_below * (wbuf[0, h, pl.ds(r, 8), :] * buf[0, h, pl.ds(r, 8), :])
+            hi = m_above * (wbuf[levels - 1, h, pl.ds(r, 8), :] * buf[levels - 1, h, pl.ds(r, 8), :])
+            ends[tile, 2 * q] = ends[tile, 2 * q] + low_value * lo
+            ends[tile, 2 * q + 1] = ends[tile, 2 * q + 1] + low_flux * lo - hi
+        dst = lax.rem(tile * stride, n)
+
+        @pl.when(dst != me)
+        def _():
+            fwd_copy(tile, me, dst).start()
+
+        @pl.when(dst == me)
+        def _():
+            gathered[me] = ends[tile]
+
+    inner = blocks - 2
+
+    def inner_step(s, carry):
+        block(s + 1)
         return carry
 
-    lax.fori_loop(0, blocks, block, 0)
+    lax.fori_loop(0, inner, inner_step, 0)
+
+    above_id = lax.rem(me + 1, n)
+    below_id = lax.rem(me + n - 1, n)
+    mat_copy(1).wait_recv()
+    mat_copy(n - 1).wait_recv()
+    m_above = jnp.where(me < n - 1, NEW_WEIGHT, 0.0) * jnp.broadcast_to(
+        mats[above_id, pl.ds(5, 1), :], (8, 128)
+    )
+    m_below = jnp.where(me > 0, NEW_WEIGHT, 0.0) * jnp.broadcast_to(
+        mats[below_id, pl.ds(6, 1), :], (8, 128)
+    )
+    inv_low = 1.0 / (one * low_s[0])
+    low_value = mine[0] * inv_low + mine[1]
+    low_flux = mine[2] * inv_low + mine[3]
+
+    def inner_send(s, carry):
+        fix_and_send(halves + lax.rem(me + s, inner * halves))
+        return carry
+
+    lax.fori_loop(0, inner * halves, inner_send, 0)
+
+    to_left.wait_recv()
+    to_right.wait_recv()
+    for k in range(levels):
+        for a, buf in enumerate((tbuf, wbuf, ubuf)):
+            for h in range(halves):
+                buf[k, h, pl.ds(PAD - 1, 1), :] = edge_lo[a, h, pl.ds(k, 1), :]
+                buf[k, h, pl.ds(PAD + rows, 1), :] = edge_hi[a, h, pl.ds(k, 1), :]
+
+    def outer_step(s, carry):
+        block(s * (blocks - 1))
+        return carry
+
+    lax.fori_loop(0, 2, outer_step, 0)
+
+    def outer_send(s, carry):
+        t = lax.rem(me + s, 2 * halves)
+        fix_and_send(jnp.where(t < halves, t, t + inner * halves))
+        return carry
+
+    lax.fori_loop(0, 2 * halves, outer_send, 0)
 
     @pl.when(me > 0)
     def _():
@@ -254,44 +321,12 @@
     def _():
         for c in down_copies:
             c.wait_recv()
-
-    m_lo = NEW_WEIGHT * met_s[0]
-    m_hi = NEW_WEIGHT * met_s[levels - 1]
-
-    def fwd_copy(step):
-        to = lax.rem(me + step, n)
-        return pltpu.make_async_remote_copy(
-            src_ref=ends.at[to],
-            dst_ref=gathered.at[me],
-            send_sem=fwd_send.at[step],
-            recv_sem=fwd_recv.at[step],
-            device_id={"gz": to},
-            device_id_type=MESH,
-        )
-
-    def tile_of(buf, tile, q):
-        r = pl.multiple_of((tile // halves) * 8, 8)
-        c = pl.multiple_of(lax.rem(tile, halves) * 128, 128)
-        return buf[q, pl.ds(r, 8), pl.ds(c, 128)]
-
-    def fix(tile):
-        for q in range(2):
-            lo = m_lo * (tile_of(below, tile, 1) * tile_of(below, tile, q))
-            hi = m_hi * (tile_of(above, tile, 1) * tile_of(above, tile, q))
-            ends[tile, 2 * q] = ends[tile, 2 * q] - mine[1] * lo + inv[levels - 1] * hi
-            ends[tile, 2 * q + 1] = ends[tile, 2 * q + 1] - mine[3] * lo + hi
-
-    for step in range(1, n):
-        fix(lax.rem(me + step, n))
-        fwd_copy(step).start()
-    fix(me)
-    gathered[me] = ends[me]
 
     for q, tend in enumerate((tend_t, tend_w)):
         tend[0] = tend[0] + met_s[0] * (below[1] * below[q])
         tend[levels - 1] = tend[levels - 1] - met_s[levels - 1] * (above[1] * above[q])
 
-    for step in range(1, n):
+    for step in range(2, n - 1):
         mat_copy(step).wait_recv()
 
     def entry_of(d, r):
@@ -313,7 +348,7 @@
     scale = 1.0 / bottom[n][0]
 
     for step in range(1, n):
-        fwd_copy(step).wait_recv()
+        fwd_copy(0, lax.rem(me + step, n), me).wait_recv()
 
     for q in range(2):
         amp = [None] * n
@@ -348,13 +383,13 @@
     for step in range(1, n):
         back_copy(step).wait_recv()
     for tile in range(n):
-        r, c = 8 * (tile // halves), 128 * (tile % halves)
-        for q in range(2):
-            lo = m_lo * (
-                below[1, pl.ds(r, 8), pl.ds(c, 128)] * below[q, pl.ds(r, 8), pl.ds(c, 128)]
-            )
-            state[2 * q, pl.ds(r, 8), pl.ds(c, 128)] = entry[tile, 2 * q]
-            state[2 * q + 1, pl.ds(r, 8), pl.ds(c, 128)] = entry[tile, 2 * q + 1] - lo
+        ib, h = tile // halves, tile % halves
+        r, c = 8 * ib, 128 * h
+        own = (tile * stride) % n
+        for q, buf in enumerate((tbuf, wbuf)):
+            lo = m_below * (wbuf[0, h, pl.ds(r + PAD, 8), :] * buf[0, h, pl.ds(r + PAD, 8), :])
+            state[2 * q, pl.ds(r, 8), pl.ds(c, 128)] = entry[own, 2 * q] + inv_low * lo
+            state[2 * q + 1, pl.ds(r, 8), pl.ds(c, 128)] = entry[own, 2 * q + 1] + lo
 
     @pl.when(me < n - 1)
     def _():
@@ -370,7 +405,7 @@
     to_right.wait_send()
     for step in range(1, n):
         mat_copy(step).wait_send()
-        fwd_copy(step).wait_send()
+        fwd_copy(0, me, lax.rem(me + step, n)).wait_send()
         back_copy(step).wait_send()
 
 

time: 31.7 us -> 29.3 us (0.924)
  Pallas kernels: 31 us -> 28.6 us
    pallas_call x1, Pallas kernels: 28.7 us -> 26.3 us  [local(): pl.pallas_call(functools.partial(exchange_kernel, n), out_shape=(cube, cu...]
where the time goes in v2:
time: 29.3 us; the launch traced here: 29.2 us
  Pallas kernels  28.6 us (98%)
  between operations  0.64 us (2%)
    pallas_call x1, Pallas kernels, local(): pl.pallas_call(functools.partial(exchange_kernel, n), out_shape=(cube, cu...  26.3 us
    pallas_call x1, Pallas kernels, local(): pl.pallas_call(finish_kernel, out_shape=(cube,) * 4, in_specs=[vmem] * 6,...  2.28 us

profile of v2, /device:TPU:1, one launch (start us, length us, event | category | flops | bytes accessed | tf_op | source)
XLA Modules:
  0.0 29.2 jit_solution(5785677608570618140)
XLA Ops:
  0.6 26.3 %exchange.1 = (f32[16,64,256]{2,1,0:T(8,128)S(1)}, f32[16,64,256]{2,1,0:T(8,128)S(1)}, f32[16,64,256]{2,1,0:T(8,128)S(1)}, f32[16,64,256]{2,1,0:T(8,128)S(1)}, f...) custom-call(f32[16,64,256]{2,1,0:T(8,128)} %temp.1, f32[16,64,256]{2,1,0:T(8,128)} %u_vel.1, ...), custom_call_target="tpu_custom_call" | custom-call | tf_op jit(solution)/shard_map/exchange/pallas_call | solution.py:452
  26.9 2.3 %finish.1 = (f32[16,64,256]{2,1,0:T(8,128)}, f32[16,64,256]{2,1,0:T(8,128)}, f32[16,64,256]{2,1,0:T(8,128)}, f32[16,64,256]{2,1,0:T(8,128)}) custom-call(f32[16,64,256]{2,1,0:T(8,128)S(1)} %get-tuple-element.10.part_t, f32[16,64,256]{2,1,0:T(8,128)S(1)} %get-tuple-element.11.part_w, f32[16,64,256]{2,1,0:T(8,128)S(1)} %get-tuple-element.12.tend_t, ...), custom_call_target="tpu_custom_call" | custom-call | tf_op jit(solution)/shard_map/finish/pallas_call | solution.py:490

commit v3 on v2

--- a/solution.py
+++ b/solution.py
@@ -14,12 +14,21 @@
 PAD = 8
 
 
+def hops(mask):
+    along_x = (0, 1, 2, 1)[(mask >> 1) & 3]
+    return 4 * (along_x + 2 * (mask >> 3)) + (mask & 1)
+
+
+def far_first(n):
+    return sorted(range(1, n), key=hops, reverse=True)
+
+
 def exchange_kernel(
     n, temp, u_vel, v_vel, w_vel, temp_old, w_old, lower, upper, metric,
     part_t, part_w, tend_t, tend_w, state, basis,
     tbuf, ubuf, wbuf, vbuf, tobuf, wobuf,
     low_s, up_s, met_s,
-    inv, mine, mats, edge_out, edge_lo, edge_hi, below, above,
+    inv, mine, mats, edge_out, edge_in, edge_part, below, above,
     ends, gathered, sols, entry,
     load_sem, scal_sem, mat_send, mat_recv, edge_send, edge_recv, wall_send, wall_recv,
     fwd_send, fwd_recv, back_send, back_recv,
@@ -53,13 +62,34 @@
             c.start()
             loads.append(c)
 
+    def clear(k, carry):
+        for buf in (tbuf, wbuf, ubuf):
+            for h in range(halves):
+                buf[k, h, pl.ds(0, PAD), :] = jnp.zeros((PAD, 128), jnp.float32)
+                buf[k, h, pl.ds(rows + PAD, PAD), :] = jnp.zeros((PAD, 128), jnp.float32)
+        return carry
+
     barrier = pltpu.get_barrier_semaphore()
-    for step in range(1, n):
-        pl.semaphore_signal(
-            barrier, inc=1, device_id={"gz": lax.rem(me + step, n)}, device_id_type=MESH
-        )
     for other in (left, right):
         pl.semaphore_signal(barrier, inc=1, device_id={"gx": other}, device_id_type=MESH)
+    for mask in far_first(n):
+        pl.semaphore_signal(
+            barrier, inc=1, device_id={"gz": jnp.bitwise_xor(me, mask)}, device_id_type=MESH
+        )
+
+    lax.fori_loop(0, levels, clear, 0)
+    for c in loads[: 3 * halves]:
+        c.wait()
+
+    def pack(k, carry):
+        for e, (row, sign) in enumerate(((PAD, -0.5), (PAD + rows - 1, 0.5))):
+            for h in range(halves):
+                weight = HORIZ_DIFF + sign * ubuf[k, h, pl.ds(row, 1), :]
+                for q, buf in enumerate((tbuf, wbuf)):
+                    edge_out[e, k, pl.ds(q * halves + h, 1), :] = weight * buf[k, h, pl.ds(row, 1), :]
+        return carry
+
+    lax.fori_loop(0, levels, pack, 0)
 
     for c in scal:
         c.wait()
@@ -91,18 +121,37 @@
 
     pl.semaphore_wait(barrier, n + 1)
 
-    def mat_copy(step):
+    to_left = pltpu.make_async_remote_copy(
+        src_ref=edge_out.at[0], dst_ref=edge_in.at[1], send_sem=edge_send.at[0], recv_sem=edge_recv.at[0],
+        device_id={"gx": left}, device_id_type=MESH,
+    )
+    to_right = pltpu.make_async_remote_copy(
+        src_ref=edge_out.at[1], dst_ref=edge_in.at[0], send_sem=edge_send.at[1], recv_sem=edge_recv.at[1],
+        device_id={"gx": right}, device_id_type=MESH,
+    )
+    to_left.start()
+    to_right.start()
+
+    def mat_copy(src, dst):
         return pltpu.make_async_remote_copy(
             src_ref=mats.at[me],
-            dst_ref=mats.at[me],
-            send_sem=mat_send.at[step],
-            recv_sem=mat_recv.at[step],
-            device_id={"gz": lax.rem(me + step, n)},
+            dst_ref=mats.at[src],
+            send_sem=mat_send.at[dst],
+            recv_sem=mat_recv.at[src],
+            device_id={"gz": dst},
             device_id_type=MESH,
         )
 
-    for step in (1, n - 1, *range(2, n - 1)):
-        mat_copy(step).start()
+    above_id = lax.rem(me + 1, n)
+    below_id = lax.rem(me + n - 1, n)
+    mat_copy(me, above_id).start()
+    mat_copy(me, below_id).start()
+    for mask in far_first(n):
+        dst = jnp.bitwise_xor(me, mask)
+
+        @pl.when(jnp.logical_and(dst != above_id, dst != below_id))
+        def _():
+            mat_copy(me, dst).start()
 
     up_copies = [
         pltpu.make_async_remote_copy(
@@ -127,16 +176,6 @@
         for i, src in enumerate((temp, w_vel))
     ]
 
-    @pl.when(me < n - 1)
-    def _():
-        for c in up_copies:
-            c.start()
-
-    @pl.when(me > 0)
-    def _():
-        for c in down_copies:
-            c.start()
-
     @pl.when(me == 0)
     def _():
         below[...] = jnp.zeros_like(below)
@@ -145,23 +184,6 @@
     def _():
         above[...] = jnp.zeros_like(above)
 
-    for c in loads[: 3 * halves]:
-        c.wait()
-    for k in range(levels):
-        for a, buf in enumerate((tbuf, wbuf, ubuf)):
-            for h in range(halves):
-                edge_out[0, a, h, pl.ds(k, 1), :] = buf[k, h, pl.ds(PAD, 1), :]
-                edge_out[1, a, h, pl.ds(k, 1), :] = buf[k, h, pl.ds(PAD + rows - 1, 1), :]
-    to_left = pltpu.make_async_remote_copy(
-        src_ref=edge_out.at[0], dst_ref=edge_hi, send_sem=edge_send.at[0], recv_sem=edge_recv.at[0],
-        device_id={"gx": left}, device_id_type=MESH,
-    )
-    to_right = pltpu.make_async_remote_copy(
-        src_ref=edge_out.at[1], dst_ref=edge_lo, send_sem=edge_send.at[1], recv_sem=edge_recv.at[1],
-        device_id={"gx": right}, device_id_type=MESH,
-    )
-    to_left.start()
-    to_right.start()
     for c in loads[3 * halves :]:
         c.wait()
 
@@ -244,7 +266,9 @@
 
     stride = 5
 
-    def fix_and_send(tile):
+    back_stride = pow(stride, -1, n)
+
+    def fix(tile):
         ib = tile // halves
         h = lax.rem(tile, halves)
         r = pl.multiple_of(ib * 8 + PAD, 8)
@@ -253,28 +277,27 @@
             hi = m_above * (wbuf[levels - 1, h, pl.ds(r, 8), :] * buf[levels - 1, h, pl.ds(r, 8), :])
             ends[tile, 2 * q] = ends[tile, 2 * q] + low_value * lo
             ends[tile, 2 * q + 1] = ends[tile, 2 * q + 1] + low_flux * lo - hi
-        dst = lax.rem(tile * stride, n)
-
-        @pl.when(dst != me)
-        def _():
-            fwd_copy(tile, me, dst).start()
-
-        @pl.when(dst == me)
-        def _():
-            gathered[me] = ends[tile]
+
+    def send(inner_tiles):
+        for mask in far_first(n):
+            dst = jnp.bitwise_xor(me, mask)
+            tile = lax.rem(dst * back_stride, n)
+            inside = jnp.logical_and(tile >= halves, tile < n - halves)
+
+            @pl.when(inside if inner_tiles else jnp.logical_not(inside))
+            def _():
+                fwd_copy(tile, me, dst).start()
 
     inner = blocks - 2
 
-    def inner_step(s, carry):
-        block(s + 1)
+    def block_step(ib, carry):
+        block(ib)
         return carry
 
-    lax.fori_loop(0, inner, inner_step, 0)
-
-    above_id = lax.rem(me + 1, n)
-    below_id = lax.rem(me + n - 1, n)
-    mat_copy(1).wait_recv()
-    mat_copy(n - 1).wait_recv()
+    lax.fori_loop(0, blocks, block_step, 0)
+
+    mat_copy(above_id, me).wait_recv()
+    mat_copy(below_id, me).wait_recv()
     m_above = jnp.where(me < n - 1, NEW_WEIGHT, 0.0) * jnp.broadcast_to(
         mats[above_id, pl.ds(5, 1), :], (8, 128)
     )
@@ -285,49 +308,58 @@
     low_value = mine[0] * inv_low + mine[1]
     low_flux = mine[2] * inv_low + mine[3]
 
-    def inner_send(s, carry):
-        fix_and_send(halves + lax.rem(me + s, inner * halves))
+    def fix_step(tile, carry):
+        fix(tile)
         return carry
 
-    lax.fori_loop(0, inner * halves, inner_send, 0)
+    lax.fori_loop(0, n, fix_step, 0)
+    send(True)
 
     to_left.wait_recv()
     to_right.wait_recv()
+    edge_y = [jnp.zeros((2 * halves, 128), jnp.float32)] * 2
+    edge_flux = list(edge_y)
     for k in range(levels):
-        for a, buf in enumerate((tbuf, wbuf, ubuf)):
+        inv_k = inv[k, pl.ds(0, 2 * halves), :]
+        for e in range(2):
+            edge_part[e, k] = edge_y[e]
+            edge_flux[e] = edge_flux[e] + (edge_y[e] - NEW_WEIGHT * edge_in[e, k])
+            edge_y[e] = edge_y[e] + edge_flux[e] * inv_k
+    for e in range(2):
+        for q in range(2):
             for h in range(halves):
-                buf[k, h, pl.ds(PAD - 1, 1), :] = edge_lo[a, h, pl.ds(k, 1), :]
-                buf[k, h, pl.ds(PAD + rows, 1), :] = edge_hi[a, h, pl.ds(k, 1), :]
-
-    def outer_step(s, carry):
-        block(s * (blocks - 1))
+                tile, row, c = h + e * (n - halves), 7 * e, q * halves + h
+                for i, value in enumerate((edge_y[e], edge_flux[e])):
+                    at = ends.at[tile, 2 * q + i, pl.ds(row, 1), :]
+                    at[...] = at[...] + value[c : c + 1]
+    send(False)
+    gathered[me] = ends[lax.rem(me * back_stride, n)]
+
+    @pl.when(me < n - 1)
+    def _():
+        for c in up_copies:
+            c.start()
+
+    @pl.when(me > 0)
+    def _():
+        for c in down_copies:
+            c.start()
+
+    def edge_rows(k, carry):
+        for e in range(2):
+            row = e * (rows - 1)
+            for q, (tend, part) in enumerate(((tend_t, part_t), (tend_w, part_w))):
+                for h in range(halves):
+                    c = q * halves + h
+                    at = (k, pl.ds(row, 1), pl.ds(h * 128, 128))
+                    tend[at] = tend[at] + edge_in[e, k, pl.ds(c, 1), :]
+                    part[at] = part[at] + edge_part[e, k, pl.ds(c, 1), :]
         return carry
 
-    lax.fori_loop(0, 2, outer_step, 0)
-
-    def outer_send(s, carry):
-        t = lax.rem(me + s, 2 * halves)
-        fix_and_send(jnp.where(t < halves, t, t + inner * halves))
-        return carry
-
-    lax.fori_loop(0, 2 * halves, outer_send, 0)
-
-    @pl.when(me > 0)
-    def _():
-        for c in up_copies:
-            c.wait_recv()
-
-    @pl.when(me < n - 1)
-    def _():
-        for c in down_copies:
-            c.wait_recv()
-
-    for q, tend in enumerate((tend_t, tend_w)):
-        tend[0] = tend[0] + met_s[0] * (below[1] * below[q])
-        tend[levels - 1] = tend[levels - 1] - met_s[levels - 1] * (above[1] * above[q])
+    lax.fori_loop(0, levels, edge_rows, 0)
 
     for step in range(2, n - 1):
-        mat_copy(step).wait_recv()
+        mat_copy(lax.rem(me + step, n), me).wait_recv()
 
     def entry_of(d, r):
         return jnp.broadcast_to(mats[d, pl.ds(r, 1), :], (8, 128))
@@ -366,22 +398,35 @@
             a, b = bottom[d + 1]
             run = run + (a * gathered[d, 2 * q + 1] - b * gathered[d, 2 * q])
 
-    def back_copy(step):
-        to = lax.rem(me + step, n)
+    def back_copy(src, dst):
         return pltpu.make_async_remote_copy(
-            src_ref=sols.at[to],
-            dst_ref=entry.at[me],
-            send_sem=back_send.at[step],
-            recv_sem=back_recv.at[step],
-            device_id={"gz": to},
+            src_ref=sols.at[dst],
+            dst_ref=entry.at[src],
+            send_sem=back_send.at[dst],
+            recv_sem=back_recv.at[src],
+            device_id={"gz": dst},
             device_id_type=MESH,
         )
 
+    for mask in far_first(n):
+        back_copy(me, jnp.bitwise_xor(me, mask)).start()
+    entry[me] = sols[me]
+    @pl.when(me > 0)
+    def _():
+        for c in up_copies:
+            c.wait_recv()
+
+    @pl.when(me < n - 1)
+    def _():
+        for c in down_copies:
+            c.wait_recv()
+
+    for q, tend in enumerate((tend_t, tend_w)):
+        tend[0] = tend[0] + met_s[0] * (below[1] * below[q])
+        tend[levels - 1] = tend[levels - 1] - met_s[levels - 1] * (above[1] * above[q])
+
     for step in range(1, n):
-        back_copy(step).start()
-    entry[me] = sols[me]
-    for step in range(1, n):
-        back_copy(step).wait_recv()
+        back_copy(lax.rem(me + step, n), me).wait_recv()
     for tile in range(n):
         ib, h = tile // halves, tile % halves
         r, c = 8 * ib, 128 * h
@@ -404,9 +449,9 @@
     to_left.wait_send()
     to_right.wait_send()
     for step in range(1, n):
-        mat_copy(step).wait_send()
+        mat_copy(me, lax.rem(me + step, n)).wait_send()
         fwd_copy(0, me, lax.rem(me + step, n)).wait_send()
-        back_copy(step).wait_send()
+        back_copy(me, lax.rem(me + step, n)).wait_send()
 
 
 def finish_kernel(
@@ -448,7 +493,7 @@
     dma = pltpu.SemaphoreType.DMA
     padded = pltpu.VMEM((levels, halves, rows + 2 * PAD, 128), f32)
     plain = pltpu.VMEM((levels, halves, rows, 128), f32)
-    edge = (3, halves, levels, 128)
+    edge = pltpu.VMEM((2, levels, 2 * halves, 128), f32)
     parts = pl.pallas_call(
         functools.partial(exchange_kernel, n),
         out_shape=(
@@ -464,9 +509,7 @@
             pltpu.VMEM((levels, 8, 128), f32),
             pltpu.VMEM((4, 8, 128), f32),
             pltpu.VMEM((n, 8, 128), f32),
-            pltpu.VMEM((2, *edge), f32),
-            pltpu.VMEM(edge, f32),
-            pltpu.VMEM(edge, f32),
+            edge, edge, edge,
             pltpu.VMEM((2, rows, cols), f32),
             pltpu.VMEM((2, rows, cols), f32),
             pltpu.VMEM((n, 4, 8, 128), f32),

time: 29.3 us -> 28.7 us (0.980)
  Pallas kernels: 28.6 us -> 28 us
    pallas_call x1, Pallas kernels: 26.3 us -> 25.7 us  [local(): pl.pallas_call(functools.partial(exchange_kernel, n), out_shape=(cube, cu...]
where the time goes in v3:
time: 28.7 us; the launch traced here: 28.6 us
  Pallas kernels  28 us (98%)
  between operations  0.64 us (2%)
    pallas_call x1, Pallas kernels, local(): pl.pallas_call(functools.partial(exchange_kernel, n), out_shape=(cube, cu...  25.7 us
    pallas_call x1, Pallas kernels, local(): pl.pallas_call(finish_kernel, out_shape=(cube,) * 4, in_specs=[vmem] * 6,...  2.28 us

profile of v3, /device:TPU:1, one launch (start us, length us, event | category | flops | bytes accessed | tf_op | source)
XLA Modules:
  0.0 28.6 jit_solution(560164403758691862)
XLA Ops:
  0.6 25.7 %exchange.1 = (f32[16,64,256]{2,1,0:T(8,128)S(1)}, f32[16,64,256]{2,1,0:T(8,128)S(1)}, f32[16,64,256]{2,1,0:T(8,128)S(1)}, f32[16,64,256]{2,1,0:T(8,128)S(1)}, f...) custom-call(f32[16,64,256]{2,1,0:T(8,128)} %temp.1, f32[16,64,256]{2,1,0:T(8,128)} %u_vel.1, ...), custom_call_target="tpu_custom_call" | custom-call | tf_op jit(solution)/shard_map/exchange/pallas_call | solution.py:497
  26.3 2.3 %finish.1 = (f32[16,64,256]{2,1,0:T(8,128)}, f32[16,64,256]{2,1,0:T(8,128)}, f32[16,64,256]{2,1,0:T(8,128)}, f32[16,64,256]{2,1,0:T(8,128)}) custom-call(f32[16,64,256]{2,1,0:T(8,128)S(1)} %get-tuple-element.10.part_t, f32[16,64,256]{2,1,0:T(8,128)S(1)} %get-tuple-element.11.part_w, f32[16,64,256]{2,1,0:T(8,128)S(1)} %get-tuple-element.12.tend_t, ...), custom_call_target="tpu_custom_call" | custom-call | tf_op jit(solution)/shard_map/finish/pallas_call | solution.py:533

commit v4 on v3

--- a/solution.py
+++ b/solution.py
@@ -28,9 +28,9 @@
     part_t, part_w, tend_t, tend_w, state, basis,
     tbuf, ubuf, wbuf, vbuf, tobuf, wobuf,
     low_s, up_s, met_s,
-    inv, mine, mats, edge_out, edge_in, edge_part, below, above,
+    inv, mine, near, edge_out, edge_in, edge_part, below, above,
     ends, gathered, sols, entry,
-    load_sem, scal_sem, mat_send, mat_recv, edge_send, edge_recv, wall_send, wall_recv,
+    load_sem, scal_sem, near_send, near_recv, edge_send, edge_recv, wall_send, wall_recv,
     fwd_send, fwd_recv, back_send, back_recv,
 ):
     levels, rows, cols = temp.shape
@@ -117,9 +117,27 @@
     mat = jnp.where(sub == 4, one * low_s[0], mat)
     mat = jnp.where(sub == 5, one * met_s[0], mat)
     mat = jnp.where(sub == 6, one * met_s[levels - 1], mat)
-    mats[me] = mat
+    near[0] = mat
+    for tile in range(n):
+        ends[tile, 4] = mat
 
     pl.semaphore_wait(barrier, n + 1)
+
+    above_id = lax.rem(me + 1, n)
+    below_id = lax.rem(me + n - 1, n)
+    near_copies = [
+        pltpu.make_async_remote_copy(
+            src_ref=near.at[0],
+            dst_ref=near.at[2 - i],
+            send_sem=near_send.at[i],
+            recv_sem=near_recv.at[1 - i],
+            device_id={"gz": other},
+            device_id_type=MESH,
+        )
+        for i, other in enumerate((above_id, below_id))
+    ]
+    for c in near_copies:
+        c.start()
 
     to_left = pltpu.make_async_remote_copy(
         src_ref=edge_out.at[0], dst_ref=edge_in.at[1], send_sem=edge_send.at[0], recv_sem=edge_recv.at[0],
@@ -131,27 +149,6 @@
     )
     to_left.start()
     to_right.start()
-
-    def mat_copy(src, dst):
-        return pltpu.make_async_remote_copy(
-            src_ref=mats.at[me],
-            dst_ref=mats.at[src],
-            send_sem=mat_send.at[dst],
-            recv_sem=mat_recv.at[src],
-            device_id={"gz": dst},
-            device_id_type=MESH,
-        )
-
-    above_id = lax.rem(me + 1, n)
-    below_id = lax.rem(me + n - 1, n)
-    mat_copy(me, above_id).start()
-    mat_copy(me, below_id).start()
-    for mask in far_first(n):
-        dst = jnp.bitwise_xor(me, mask)
-
-        @pl.when(jnp.logical_and(dst != above_id, dst != below_id))
-        def _():
-            mat_copy(me, dst).start()
 
     up_copies = [
         pltpu.make_async_remote_copy(
@@ -296,13 +293,13 @@
 
     lax.fori_loop(0, blocks, block_step, 0)
 
-    mat_copy(above_id, me).wait_recv()
-    mat_copy(below_id, me).wait_recv()
+    for c in near_copies:
+        c.wait_recv()
     m_above = jnp.where(me < n - 1, NEW_WEIGHT, 0.0) * jnp.broadcast_to(
-        mats[above_id, pl.ds(5, 1), :], (8, 128)
+        near[1, pl.ds(5, 1), :], (8, 128)
     )
     m_below = jnp.where(me > 0, NEW_WEIGHT, 0.0) * jnp.broadcast_to(
-        mats[below_id, pl.ds(6, 1), :], (8, 128)
+        near[2, pl.ds(6, 1), :], (8, 128)
     )
     inv_low = 1.0 / (one * low_s[0])
     low_value = mine[0] * inv_low + mine[1]
@@ -358,11 +355,11 @@
 
     lax.fori_loop(0, levels, edge_rows, 0)
 
-    for step in range(2, n - 1):
-        mat_copy(lax.rem(me + step, n), me).wait_recv()
+    for step in range(1, n):
+        fwd_copy(0, lax.rem(me + step, n), me).wait_recv()
 
     def entry_of(d, r):
-        return jnp.broadcast_to(mats[d, pl.ds(r, 1), :], (8, 128))
+        return jnp.broadcast_to(gathered[d, 4, pl.ds(r, 1), :], (8, 128))
 
     bottom = [(one, entry_of(0, 4))]
     for d in range(n):
@@ -378,9 +375,6 @@
         )
     top = top[::-1]
     scale = 1.0 / bottom[n][0]
-
-    for step in range(1, n):
-        fwd_copy(0, lax.rem(me + step, n), me).wait_recv()
 
     for q in range(2):
         amp = [None] * n
@@ -446,10 +440,9 @@
         for c in down_copies:
             c.wait_send()
 
-    to_left.wait_send()
-    to_right.wait_send()
+    for c in (to_left, to_right, *near_copies):
+        c.wait_send()
     for step in range(1, n):
-        mat_copy(me, lax.rem(me + step, n)).wait_send()
         fwd_copy(0, me, lax.rem(me + step, n)).wait_send()
         back_copy(me, lax.rem(me + step, n)).wait_send()
 
@@ -508,16 +501,16 @@
             pltpu.SMEM((levels,), f32), pltpu.SMEM((levels,), f32), pltpu.SMEM((levels,), f32),
             pltpu.VMEM((levels, 8, 128), f32),
             pltpu.VMEM((4, 8, 128), f32),
-            pltpu.VMEM((n, 8, 128), f32),
+            pltpu.VMEM((3, 8, 128), f32),
             edge, edge, edge,
             pltpu.VMEM((2, rows, cols), f32),
             pltpu.VMEM((2, rows, cols), f32),
-            pltpu.VMEM((n, 4, 8, 128), f32),
-            pltpu.VMEM((n, 4, 8, 128), f32),
+            pltpu.VMEM((n, 5, 8, 128), f32),
+            pltpu.VMEM((n, 5, 8, 128), f32),
             pltpu.VMEM((n, 4, 8, 128), f32),
             pltpu.VMEM((n, 4, 8, 128), f32),
             dma((6, halves)), dma((3,)),
-            dma((n,)), dma((n,)), dma((2,)), dma((2,)), dma((2, 2)), dma((2, 2)),
+            dma((2,)), dma((2,)), dma((2,)), dma((2,)), dma((2, 2)), dma((2, 2)),
             dma((n,)), dma((n,)), dma((n,)), dma((n,)),
         ],
         compiler_params=pltpu.CompilerParams(

time: 28.7 us -> 28.6 us (level)
  no operation moved by 1% of the time
where the time goes in v4:
time: 28.6 us; the launch traced here: 28.5 us
  Pallas kernels  27.9 us (98%)
  between operations  0.64 us (2%)
    pallas_call x1, Pallas kernels, local(): pl.pallas_call(functools.partial(exchange_kernel, n), out_shape=(cube, cu...  25.6 us
    pallas_call x1, Pallas kernels, local(): pl.pallas_call(finish_kernel, out_shape=(cube,) * 4, in_specs=[vmem] * 6,...  2.28 us

profile of v4, /device:TPU:1, one launch (start us, length us, event | category | flops | bytes accessed | tf_op | source)
XLA Modules:
  0.0 28.5 jit_solution(11527788957710070986)
XLA Ops:
  0.6 25.6 %exchange.1 = (f32[16,64,256]{2,1,0:T(8,128)S(1)}, f32[16,64,256]{2,1,0:T(8,128)S(1)}, f32[16,64,256]{2,1,0:T(8,128)S(1)}, f32[16,64,256]{2,1,0:T(8,128)S(1)}, f...) custom-call(f32[16,64,256]{2,1,0:T(8,128)} %temp.1, f32[16,64,256]{2,1,0:T(8,128)} %u_vel.1, ...), custom_call_target="tpu_custom_call" | custom-call | tf_op jit(solution)/shard_map/exchange/pallas_call | solution.py:490
  26.3 2.3 %finish.1 = (f32[16,64,256]{2,1,0:T(8,128)}, f32[16,64,256]{2,1,0:T(8,128)}, f32[16,64,256]{2,1,0:T(8,128)}, f32[16,64,256]{2,1,0:T(8,128)}) custom-call(f32[16,64,256]{2,1,0:T(8,128)S(1)} %get-tuple-element.10.part_t, f32[16,64,256]{2,1,0:T(8,128)S(1)} %get-tuple-element.11.part_w, f32[16,64,256]{2,1,0:T(8,128)S(1)} %get-tuple-element.12.tend_t, ...), custom_call_target="tpu_custom_call" | custom-call | tf_op jit(solution)/shard_map/finish/pallas_call | solution.py:526
